TPU v7x, 32 devices: a whole 2x2x4 slice. The times are simulated.
32 devices in a mesh: frames: 2 (over x), date: 8 (over z, y), row: 2 (over core).
Axes of the slice: x: 2, y: 2, z: 4, core: 2. Of those that a mesh axis runs over, the one named last changes fastest.
Arguments:
- intensity: float32 [128, 512, 512], P(('frames', 'date'), 'row'), parts along dimension 0, may hold values from 0.05 to 20
Outputs:
- filtered: float32 [128, 512, 512], P(('frames', 'date'), 'row'), parts along dimension 0
- change: float32 [128, 512, 512], P(('frames', 'date'), 'row'), parts along dimension 0
There are 2 independent parts, one for each index of `frames`. A program takes and returns all parts, laid end to end along the dimension named above; each array names one. Nothing has to cross between parts.
All inputs are finite; a program needn't handle non-finite values.
Results may differ from a plain program's by a relative error of at most 0.00002.
Values sent between devices are 32-bit elements; how exact they have to be, the bound alone decides.
A program may use at most 64 MiB of HBM per device.

v0:
```python
import jax
import jax.numpy as jnp
from jax import lax
from jax.sharding import PartitionSpec as P

RADIUS = 3


def padded_2(cells, sides, width):
    for axis, dim in sides:
        count = lax.axis_size(axis)
        ends = count - 1
        head = lax.slice_in_dim(cells, 0, width, axis=dim)
        tail = lax.slice_in_dim(cells, cells.shape[dim] - width, cells.shape[dim], axis=dim)
        cells = jnp.concatenate(
            [
                lax.ppermute(tail, axis, [(i, (i + 1) % count) for i in range(ends)]),
                cells,
                lax.ppermute(head, axis, [((i + 1) % count, i) for i in range(ends)]),
            ],
            axis=dim,
        )
    return cells


def shifted(block, axis, distance):
    devices = range(lax.axis_size(axis))
    route = [(i - distance, i) for i in devices if i - distance in devices]
    return lax.ppermute(block, axis, route)


def rim_sum(haloed, rows_n):
    width = 2 * RADIUS + 1
    cols_n = haloed.shape[2]
    padded = jnp.pad(haloed, ((0, 0), (0, 0), (RADIUS, RADIUS)))
    across = padded[:, 0:rows_n, :]
    for offset in range(1, width):
        across = across + padded[:, offset : offset + rows_n, :]
    total = across[:, :, 0:cols_n]
    for offset in range(1, width):
        total = total + across[:, :, offset : offset + cols_n]
    return total


def valid_count(first, length, extent):
    places = first + jnp.arange(length, dtype=jnp.int32)
    counted = jnp.zeros((length,), jnp.float32)
    for offset in range(-RADIUS, RADIUS + 1):
        inside = (places + offset >= 0) & (places + offset < extent)
        counted = counted + inside.astype(jnp.float32)
    return counted


def on_device(intensity):
    rows_n = intensity.shape[1]
    cols_n = intensity.shape[2]
    row_groups = lax.axis_size("row")
    date_groups = lax.axis_size("date")
    total_dates = intensity.shape[0] * date_groups
    row_first = lax.axis_index("row") * rows_n
    row_count = valid_count(row_first, rows_n, rows_n * row_groups)
    col_count = valid_count(jnp.int32(0), cols_n, cols_n)
    count = row_count[:, None] * col_count[None, :]
    haloed = padded_2(intensity, (("row", 1),), RADIUS)
    local_mean = rim_sum(haloed, rows_n) / count[None]
    is_last = lax.axis_index("date") == date_groups - 1
    ratio_sum = lax.psum(jnp.sum(intensity / local_mean, axis=0), "date")
    scale = ratio_sum[None] / jnp.float32(total_dates)
    filtered = local_mean * scale
    following = shifted(haloed[0:1], "date", -1)
    follow_mean = rim_sum(following, rows_n) / count[None]
    successor = jnp.where(is_last, filtered[-1:], follow_mean * scale)
    logged = jnp.log(filtered)
    ahead = jnp.concatenate([logged[1:], jnp.log(successor)], axis=0)
    change = ahead - logged
    return (filtered, change)


def solution(mesh):
    return jax.shard_map(
        on_device,
        mesh=mesh,
        in_specs=(P(("frames", "date"), "row", None),),
        out_specs=(P(("frames", "date"), "row", None), P(("frames", "date"), "row", None)),
        check_vma=False,
    )
```

profile of v0, /device:TPU:0, one launch (start us, length us, event | category | flops | bytes accessed | tf_op | source)
XLA Modules:
  0.0 132.5 jit_solution(6093644278905989527)
XLA Ops:
  7.2 0.0 all-reduce.4.cloned.1.call-start
  7.2 1.0 fusion.42
  8.2 2.4 %collective-permute-start = (f32[8,3,512]{2,1,0:T(4,128)S(1)}, f32[8,3,512]{2,1,0:T(4,128)S(1)}, u32[]{:S(2)}, u32[]{:S(2)}) collective-permute-start(f32[8,3,512]{2,1,0:T(4,128)S(1)} %get-tuple-element.6), channel_id=1, source_target_pairs={{0,1},{2,3},{4,5},{6,7},{8,9},{10,11},{12,13},{14,15},{16,17},{18,... | collective-permute-start | bytes 147464 | tf_op jit(solution)/shard_map/ppermute | solution.py:17
  10.6 1.3 collective-permute-start.1
  12.0 0.1 broadcast_multiply_fusion.1
  12.1 0.0 collective-permute-done
  12.1 1.7 %collective-permute-done.1 = f32[8,3,512]{2,1,0:T(4,128)S(1)} collective-permute-done((f32[8,3,512]{2,1,0:T(4,128)S(1)}, f32[8,3,512]{2,1,0:T(4,128)S(1)}, u32[]{:S(2)}, u32[]{:S(2)}) %collective-permute-start.1) | collective-permute-done | bytes 49184 | tf_op jit(solution)/shard_map/ppermute | solution.py:19
  13.8 2.8 %pad_maximum_fusion = f32[8,262,512]{2,1,0:T(8,128)S(1)} fusion(f32[8,3,512]{2,1,0:T(4,128)S(1)} %collective-permute-done.1, f32[8,256,512]{2,1,0:T(8,128)} %param.1, f32[8,3,512]{2,1,0:T(4,128)S(1)} %collective-permute-done), kind=kLoop, calls=%fused_computation.13 | loop fusion | flops 2146304 | bytes 8585216 | tf_op jit(solution)/shard_map/concatenate | solution.py:15
  16.5 0.0 copy-start
  16.5 11.3 %fusion.5 = f32[8,256,518]{2,1,0:T(8,128)S(1)} fusion(f32[8,262,512]{2,1,0:T(8,128)S(1)} %pad_maximum_fusion), kind=kLoop, calls=%fused_computation.12 | loop fusion | flops 6365184 | bytes 8536064 | tf_op jit(solution)/shard_map/add | solution.py:38
  27.9 0.0 copy-done
  27.9 10.4 %fusion.6 = (f32[256,512]{1,0:T(8,128)}, f32[8,256,512]{2,1,0:T(8,128)}) fusion(f32[8,256,512]{2,1,0:T(8,128)} %param.1, f32[256,512]{1,0:T(8,128)S(1)} %broadcast_multiply_fusion.1, f32[8,256,518]{2,1,0:T(8,128)S(1)} %fusion.5), kind=kLoop, calls=%fused_computation.23 | loop fusion | flops 9306112 | bytes 38797312 | tf_op jit(solution)/shard_map/reduce_sum | solution.py:67
  38.3 0.0 all-reduce.4.cloned.1.call-update
  38.3 1.1 slice.141
  39.4 1.5 %collective-permute-start.2 = (f32[1,262,512]{2,1,0:T(8,128)S(1)}, f32[1,262,512]{2,1,0:T(8,128)S(1)}, u32[]{:S(2)}, u32[]{:S(2)}) collective-permute-start(f32[1,262,512]{2,1,0:T(8,128)S(1)} %slice.141), channel_id=1, source_target_pairs={{2,0},{4,2},{6,4},{8,6},{10,8},{12,10},{14,12},{3,1},{5,3},{7,5},{... | collective-permute-start | bytes 1609736 | tf_op jit(solution)/shard_map/ppermute | solution.py:29
  40.9 74.4 %all-reduce.4.cloned.1.call-done = f32[256,512]{1,0:T(8,128)} async-done(((f32[256,512]{1,0:T(8,128)}), f32[256,512]{1,0:T(8,128)}) %all-reduce.4.cloned.1.call-update) | async-done | bytes 524304 | tf_op jit(solution)/shard_map/psum | solution.py:67
  115.3 1.1 broadcast_multiply_fusion
  116.4 3.3 %fusion.41 = (f32[8,256,512]{2,1,0:T(8,128)S(1)}, f32[8,256,512]{2,1,0:T(8,128)S(1)}) fusion(f32[256,512]{1,0:T(8,128)S(1)} %broadcast_multiply_fusion, f32[8,256,512]{2,1,0:T(8,128)} %get-tuple-element.5, f32[256,512]{1,0:T(8,128)S(1)} %broadcast_multiply_fusion.1), kind=kLoop, calls=%fused_computation.88 | loop fusion | flops 2097152 | bytes 13631488 | tf_op jit(solution)/shard_map/log | solution.py:73
  119.7 0.0 copy-start.1
  119.7 0.0 copy-start.2
  119.7 0.5 slice.139
  120.3 0.0 collective-permute-done.2
  120.3 1.4 %fusion.12 = f32[1,256,518]{2,1,0:T(8,128)S(1)} fusion(f32[1,262,512]{2,1,0:T(8,128)S(1)} %collective-permute-done.2), kind=kLoop, calls=%fused_computation.36 | loop fusion | flops 795648 | bytes 1067008 | tf_op jit(solution)/shard_map/add | solution.py:38
  121.7 0.0 copy-done.2
  121.7 0.9 fusion.16
  122.6 0.0 copy-done.1
  122.6 3.0 %maximum_subtract_fusion = f32[8,256,512]{2,1,0:T(8,128)} fusion(f32[1,256,512]{2,1,0:T(8,128)S(1)} %fusion.16, f32[7,256,512]{2,1,0:T(8,128)S(1)} %slice.139, f32[8,256,512]{2,1,0:T(8,128)S(1)} %get-tuple-element.3), kind=kLoop, calls=%fused_computation.20 | loop fusion | flops 2097152 | bytes 12582912 | tf_op jit(solution)/shard_map/sub | solution.py:75
  (2 shorter events, 0.0 us)
Async XLA Ops:
  7.2 108.1 %all-reduce.4.cloned.1.call-start = ((), (), s32[]{:S(2)}) async-start(), calls=%async_computation | async-start | bytes 1048576 | tf_op jit(solution)/shard_map/psum | solution.py:67
  8.2 3.9 %collective-permute-start = (f32[8,3,512]{2,1,0:T(4,128)S(1)}, f32[8,3,512]{2,1,0:T(4,128)S(1)}, u32[]{:S(2)}, u32[]{:S(2)}) collective-permute-start(f32[8,3,512]{2,1,0:T(4,128)S(1)} %get-tuple-element.6), channel_id=1, source_target_pairs={{0,1},{2,3},{4,5},{6,7},{8,9},{10,11},{12,13},{14,15},{16,17},{18,... | collective-permute-start | bytes 147464 | tf_op jit(solution)/shard_map/ppermute | solution.py:17
  10.6 3.1 %collective-permute-start.1 = (f32[8,3,512]{2,1,0:T(4,128)S(1)}, f32[8,3,512]{2,1,0:T(4,128)S(1)}, u32[]{:S(2)}, u32[]{:S(2)}) collective-permute-start(f32[8,3,512]{2,1,0:T(4,128)S(1)} %get-tuple-element.7), channel_id=1, source_target_pairs={{1,0},{3,2},{5,4},{7,6},{9,8},{11,10},{13,12},{15,14},{17,16},{19,... | collective-permute-start | bytes 147464 | tf_op jit(solution)/shard_map/ppermute | solution.py:19
  16.5 11.3 %copy-start = (f32[8,262,512]{2,1,0:T(8,128)}, f32[8,262,512]{2,1,0:T(8,128)S(1)}, u32[]{:S(2)}) copy-start(f32[8,262,512]{2,1,0:T(8,128)S(1)} %pad_maximum_fusion) | copy-start | bytes 12877828
  39.4 80.9 %collective-permute-start.2 = (f32[1,262,512]{2,1,0:T(8,128)S(1)}, f32[1,262,512]{2,1,0:T(8,128)S(1)}, u32[]{:S(2)}, u32[]{:S(2)}) collective-permute-start(f32[1,262,512]{2,1,0:T(8,128)S(1)} %slice.141), channel_id=1, source_target_pairs={{2,0},{4,2},{6,4},{8,6},{10,8},{12,10},{14,12},{3,1},{5,3},{7,5},{... | collective-permute-start | bytes 1609736 | tf_op jit(solution)/shard_map/ppermute | solution.py:29
  119.7 3.0 %copy-start.1 = (f32[8,256,512]{2,1,0:T(8,128)}, f32[8,256,512]{2,1,0:T(8,128)S(1)}, u32[]{:S(2)}) copy-start(f32[8,256,512]{2,1,0:T(8,128)S(1)} %get-tuple-element.3) | copy-start | bytes 12582916
  119.7 2.0 %copy-start.2 = (f32[256,512]{1,0:T(8,128)S(1)}, f32[256,512]{1,0:T(8,128)}, u32[]{:S(2)}) copy-start(f32[256,512]{1,0:T(8,128)} %all-reduce.4.cloned.1.call-done) | copy-start | bytes 1572868
Sparse Core Ops, SparseCore 0:
  38.4 76.8 all-reduce.3
where the time goes:
time: 133 us
  waiting for transfers between devices  76.1 us (57%)
  other arithmetic  34.4 us (26%)
  between operations  14.2 us (11%)
  starting transfers between devices  5.2 us (4%)
  local copies, waits for them, and re-layouts  2.64 us (2%)
    psum x1, waiting for transfers between devices, on_device(): ratio_sum = lax.psum(jnp.sum(intensity / local_mean, axis=0), 'date')  74.4 us
    add x2, other arithmetic, rim_sum(): across = across + padded[:, offset:offset + rows_n, :]  12.7 us
    reduce_sum x1, other arithmetic, on_device(): ratio_sum = lax.psum(jnp.sum(intensity / local_mean, axis=0), 'date')  10.4 us
    log x1, other arithmetic, on_device(): logged = jnp.log(filtered)  3.32 us
    sub x1, other arithmetic, on_device(): change = ahead - logged  3.05 us
    concatenate x1, other arithmetic, padded_2(): jnp.concatenate([lax.ppermute(tail, axis, [(i, (i + 1) % count) for i in...  2.75 us
  transfers between devices with their start and end apart: 4, of which 2 were waited for; matrix products, arithmetic and copies ran while one was open for 5% of the time, Pallas kernels for 0%

commit v1 on v0

v1 whole, which is shorter than its diff:
```python
import functools

import jax
import jax.numpy as jnp
from jax import lax
from jax.experimental import pallas as pl
from jax.experimental.pallas import tpu as pltpu
from jax.sharding import PartitionSpec as P

RADIUS = 3
RIM = 8
CHUNK = 32
MESH = pl.DeviceIdType.MESH
NEAR = ((0, 1), (0, -1), (1, 0), (-1, 0), (1, 1), (1, -1), (-1, 1), (-1, -1), (2, 0), (-2, 0))


def band_rows(block, rows):
    n = block.shape[0]
    three = block + pltpu.roll(block, 1, 0) + pltpu.roll(block, 2, 0)
    four = three + pltpu.roll(block, 3, 0)
    return (four + pltpu.roll(three, n - 3, 0))[RIM : RIM + rows]


def band_cols(block):
    n = block.shape[1]
    wide = jnp.concatenate([block, jnp.zeros((block.shape[0], 128), block.dtype)], axis=1)
    m = wide.shape[1]
    three = wide + pltpu.roll(wide, 1, 1) + pltpu.roll(wide, 2, 1)
    four = three + pltpu.roll(wide, 3, 1)
    return (four + pltpu.roll(three, m - 3, 1))[:, :n]


def span(place, extent):
    low = jnp.maximum(place - RADIUS, 0)
    high = jnp.minimum(place + RADIUS, extent - 1)
    return (high - low + 1).astype(jnp.float32)


def comm_kernel(dates_n, rows_n_groups, x, lm_out, tot_out, nxt_out,
                xv, sv, lmv, part, rsb, own, buf, fwd, tot, nxt,
                load_sem, rim_s, rim_r, suc_s, suc_r, rs_s, rs_r, sc_s, sc_r,
                ag_s, ag_r, out_sem):
    t_n, rows, cols = x.shape
    half = rows // 2
    n_half = half // CHUNK
    line = dates_n // 2
    d = lax.axis_index("date")
    r = lax.axis_index("row")
    a, b = d // 2, d % 2
    pair = d + 1 - 2 * b
    up_row, down_row = r > 0, r < rows_n_groups - 1
    has_next, has_prev = d < dates_n - 1, d > 0

    loads = [
        pltpu.make_async_copy(x.at[t], xv.at[t, pl.ds(RIM, rows)], load_sem.at[t])
        for t in range(t_n)
    ]
    for c in loads:
        c.start()

    barrier = pltpu.get_barrier_semaphore()
    expect = 0
    for dd, dr in NEAR:
        there = (d + dd >= 0) & (d + dd < dates_n) & (r + dr >= 0) & (r + dr < rows_n_groups)

        @pl.when(there)
        def _():
            pl.semaphore_signal(barrier, inc=1, device_id={"date": d + dd, "row": r + dr},
                                device_id_type=MESH)

        expect = expect + jnp.where(there, 1, 0)

    zero_rim = jnp.zeros((t_n, RIM, cols), jnp.float32)

    @pl.when(jnp.logical_not(up_row))
    def _():
        xv[:, 0:RIM, :] = zero_rim
        sv[0:RIM, :] = zero_rim[0]

    @pl.when(jnp.logical_not(down_row))
    def _():
        xv[:, RIM + rows :, :] = zero_rim
        sv[RIM + rows :, :] = zero_rim[0]

    @pl.when(a == 0)
    def _():
        buf[0] = jnp.zeros(buf.shape[1:], jnp.float32)

    @pl.when(a == line - 1)
    def _():
        buf[1] = jnp.zeros(buf.shape[1:], jnp.float32)

    pl.semaphore_wait(barrier, expect)

    def remote(src, dst, s, q, date, row):
        return pltpu.make_async_remote_copy(
            src_ref=src, dst_ref=dst, send_sem=s, recv_sem=q,
            device_id={"date": date, "row": row}, device_id_type=MESH)

    rim_down = remote(x.at[:, pl.ds(rows - RIM, RIM)], xv.at[:, pl.ds(0, RIM)],
                      rim_s.at[0], rim_r.at[0], d, r + 1)
    rim_up = remote(x.at[:, pl.ds(0, RIM)], xv.at[:, pl.ds(RIM + rows, RIM)],
                    rim_s.at[1], rim_r.at[1], d, r - 1)

    @pl.when(down_row)
    def _():
        rim_down.start()

    @pl.when(up_row)
    def _():
        rim_up.start()

    n_suc = 4
    piece = rows // n_suc
    suc = [
        remote(x.at[0, pl.ds(i * piece, piece)], sv.at[pl.ds(RIM + i * piece, piece)],
               suc_s.at[i], suc_r.at[i], d - 1, r)
        for i in range(n_suc)
    ]
    suc_down = remote(x.at[0, pl.ds(rows - RIM, RIM)], sv.at[pl.ds(0, RIM)],
                      suc_s.at[n_suc], suc_r.at[n_suc], d - 1, r + 1)
    suc_up = remote(x.at[0, pl.ds(0, RIM)], sv.at[pl.ds(RIM + rows, RIM)],
                    suc_s.at[n_suc + 1], suc_r.at[n_suc + 1], d - 1, r - 1)

    @pl.when(has_prev)
    def _():
        suc[0].start()
        suc[1].start()

    for c in loads:
        c.wait()

    @pl.when(up_row)
    def _():
        rim_down.wait_recv()

    @pl.when(down_row)
    def _():
        rim_up.wait_recv()

    def inverse(base):
        row = lax.broadcasted_iota(jnp.int32, (CHUNK, cols), 0) + (base + r * rows)
        col = lax.broadcasted_iota(jnp.int32, (CHUNK, cols), 1)
        return 1.0 / (span(row, rows * rows_n_groups) * span(col, cols))

    def ratios(base):
        inv = inverse(base)

        def one(t, acc):
            block = xv[t, pl.ds(base, CHUNK + 2 * RIM), :]
            mean = band_cols(band_rows(block, CHUNK)) * inv
            lmv[t, pl.ds(base, CHUNK), :] = mean
            return acc + block[RIM : RIM + CHUNK] / mean

        acc = lax.fori_loop(0, t_n, one, jnp.zeros((CHUNK, cols), jnp.float32))
        part[pl.ds(base, CHUNK), :] = acc

    def away(k):
        return pl.multiple_of((1 - b) * half + k * CHUNK, CHUNK)

    def mine(k):
        return pl.multiple_of(b * half + k * CHUNK, CHUNK)

    def rs_copy(k):
        return remote(part.at[pl.ds(away(k), CHUNK)], rsb.at[k], rs_s.at[k], rs_r.at[k], pair, r)

    def first_half(k, _):
        ratios(away(k))
        rs_copy(k).start()
        return 0

    lax.fori_loop(0, n_half, first_half, 0)

    @pl.when(has_prev)
    def _():
        suc[2].start()
        suc[3].start()

        @pl.when(down_row)
        def _():
            suc_down.start()

        @pl.when(up_row)
        def _():
            suc_up.start()

    def second_half(k, _):
        ratios(mine(k))
        return 0

    lax.fori_loop(0, n_half, second_half, 0)

    mean_out = pltpu.make_async_copy(lmv, lm_out, out_sem.at[0])
    mean_out.start()

    lead = jnp.where(a >= line // 2, 1, 0)

    def scan_copy(way, k):
        return remote(fwd.at[way, k], buf.at[way, k], sc_s.at[way, k], sc_r.at[way, k],
                      d + 2 - 4 * way, r)

    def came(way):
        return jnp.where(way == 0, a, line - 1 - a) > 0

    def goes(way):
        return jnp.where(way == 0, line - 1 - a, a) > 0

    def scan(way, k):
        @pl.when(came(way))
        def _():
            scan_copy(way, k).wait_recv()

        @pl.when(goes(way))
        def _():
            fwd[way, k] = own[k] + buf[way, k]
            scan_copy(way, k).start()

    def ag_copy(k):
        place = pl.ds(mine(k), CHUNK)
        return remote(tot.at[place], tot.at[place], ag_s.at[k], ag_r.at[k], pair, r)

    skew = 2
    for i in range(n_half + skew):
        if i < n_half:
            rs_copy(i).wait_recv()
            own[i] = part[pl.ds(mine(i), CHUNK), :] + rsb[i]
            scan(lead, i)
        k = i - skew
        if k >= 0:
            scan(1 - lead, k)
            tot[pl.ds(mine(k), CHUNK), :] = buf[0, k] + own[k] + buf[1, k]
            ag_copy(k).start()

    @pl.when(has_next)
    def _():
        for c in suc:
            c.wait_recv()

        @pl.when(up_row)
        def _():
            suc_down.wait_recv()

        @pl.when(down_row)
        def _():
            suc_up.wait_recv()

        def after(k, _):
            base = pl.multiple_of(k * CHUNK, CHUNK)
            block = sv[pl.ds(base, CHUNK + 2 * RIM), :]
            nxt[pl.ds(base, CHUNK), :] = band_cols(band_rows(block, CHUNK)) * inverse(base)
            return 0

        lax.fori_loop(0, rows // CHUNK, after, 0)

    @pl.when(jnp.logical_not(has_next))
    def _():
        nxt[...] = lmv[t_n - 1]

    nxt_copy = pltpu.make_async_copy(nxt, nxt_out, out_sem.at[1])
    nxt_copy.start()

    def ag_arrival(k):
        place = pl.ds(away(k), CHUNK)
        return remote(tot.at[place], tot.at[place], ag_s.at[k], ag_r.at[k], pair, r)

    for k in range(n_half):
        ag_arrival(k).wait_recv()
    tot_copy = pltpu.make_async_copy(tot, tot_out, out_sem.at[2])
    tot_copy.start()

    @pl.when(down_row)
    def _():
        rim_down.wait_send()

    @pl.when(up_row)
    def _():
        rim_up.wait_send()

    @pl.when(has_prev)
    def _():
        for c in suc:
            c.wait_send()

        @pl.when(down_row)
        def _():
            suc_down.wait_send()

        @pl.when(up_row)
        def _():
            suc_up.wait_send()

    for k in range(n_half):
        rs_copy(k).wait_send()
        ag_copy(k).wait_send()
        for way in range(2):

            @pl.when(goes(way))
            def _():
                scan_copy(way, k).wait_send()

    mean_out.wait()
    nxt_copy.wait()
    tot_copy.wait()


def out_kernel(total_dates, lm, tot, nxt, filtered, change):
    t_n = lm.shape[0]
    scale = tot[...] / jnp.float32(total_dates)
    ahead = jnp.log(nxt[...] * scale)
    for t in range(t_n - 1, -1, -1):
        value = lm[t] * scale
        filtered[t] = value
        logged = jnp.log(value)
        change[t] = ahead - logged
        ahead = logged


def on_device(date_groups, row_groups, intensity):
    t_n, rows, cols = intensity.shape
    f32 = jnp.float32
    n_half = rows // 2 // CHUNK
    vm = lambda *s: pltpu.VMEM(s, f32)
    dma = pltpu.SemaphoreType.DMA
    hbm = pl.BlockSpec(memory_space=pl.ANY)
    lm, tot, nxt = pl.pallas_call(
        functools.partial(comm_kernel, date_groups, row_groups),
        out_shape=(
            jax.ShapeDtypeStruct((t_n, rows, cols), f32),
            jax.ShapeDtypeStruct((rows, cols), f32),
            jax.ShapeDtypeStruct((rows, cols), f32),
        ),
        in_specs=[hbm],
        out_specs=(hbm, hbm, hbm),
        scratch_shapes=[
            vm(t_n, rows + 2 * RIM, cols),
            vm(rows + 2 * RIM, cols),
            vm(t_n, rows, cols),
            vm(rows, cols),
            vm(n_half, CHUNK, cols),
            vm(n_half, CHUNK, cols),
            vm(2, n_half, CHUNK, cols),
            vm(2, n_half, CHUNK, cols),
            vm(rows, cols),
            vm(rows, cols),
            dma((t_n,)), dma((2,)), dma((2,)), dma((6,)), dma((6,)),
            dma((n_half,)), dma((n_half,)), dma((2, n_half)), dma((2, n_half)),
            dma((n_half,)), dma((n_half,)), dma((3,)),
        ],
        compiler_params=pltpu.CompilerParams(collective_id=0, has_side_effects=True),
        name="comm",
    )(intensity)
    step = 32
    big = pl.BlockSpec((t_n, step, cols), lambda i: (0, i, 0))
    flat = pl.BlockSpec((step, cols), lambda i: (i, 0))
    return pl.pallas_call(
        functools.partial(out_kernel, t_n * date_groups),
        grid=(rows // step,),
        out_shape=(
            jax.ShapeDtypeStruct((t_n, rows, cols), f32),
            jax.ShapeDtypeStruct((t_n, rows, cols), f32),
        ),
        in_specs=[big, flat, flat],
        out_specs=(big, big),
        name="finish",
    )(lm, tot, nxt)


def solution(mesh):
    spec = P(("frames", "date"), "row", None)
    return jax.shard_map(
        functools.partial(on_device, mesh.shape["date"], mesh.shape["row"]),
        mesh=mesh,
        in_specs=(spec,),
        out_specs=(spec, spec),
        check_vma=False,
    )
```

time: 133 us -> 53.1 us (0.40)
  waiting for transfers between devices: 76.1 us -> 0 us
  Pallas kernels: 0 us -> 52.2 us
  other arithmetic: 34.4 us -> 0 us
  between operations: 14.2 us -> 0.64 us
  starting transfers between devices: 5.2 us -> 0 us
  local copies, waits for them, and re-layouts: 2.64 us -> 0 us
    psum x1 -> x0, waiting for transfers between devices: 74.4 us -> none  [on_device(): ratio_sum = lax.psum(jnp.sum(intensity / local_mean, axis=0), 'date')]
    pallas_call x0 -> x2, Pallas kernels: none -> 52.2 us  [the longest x1 44.4 us: on_device(): pl.pallas_call(functools.partial(comm_kernel, date_groups, row_groups), o...]
    add x4 -> x0, other arithmetic: 12.7 us -> none  [the longest x2 12.7 us: rim_sum(): across = across + padded[:, offset:offset + rows_n, :]]
    reduce_sum x1 -> x0, other arithmetic: 10.4 us -> none  [on_device(): ratio_sum = lax.psum(jnp.sum(intensity / local_mean, axis=0), 'date')]
    ppermute x3 -> x0, starting transfers between devices: 5.16 us -> none  [the longest x1 2.4 us: padded_2(): lax.ppermute(tail, axis, [(i, (i + 1) % count) for i in range(ends)])]
    log x2 -> x0, other arithmetic: 4.25 us -> none  [the longest x1 3.32 us: on_device(): logged = jnp.log(filtered)]
    sub x1 -> x0, other arithmetic: 3.05 us -> none  [on_device(): change = ahead - logged]
    concatenate x1 -> x0, other arithmetic: 2.75 us -> none  [padded_2(): jnp.concatenate([lax.ppermute(tail, axis, [(i, (i + 1) % count) for i in...]
  transfers between devices with their start and end apart: 4 -> 0, of which waited for: 2 -> 0; matrix products, arithmetic and copies ran while one was open for 5% -> 0% of each run, Pallas kernels for 0% -> 0%
where the time goes in v1:
time: 53.1 us; the launch traced here: 52.8 us
  Pallas kernels  52.2 us (98%)
  between operations  0.64 us (1%)
    pallas_call x1, Pallas kernels, on_device(): pl.pallas_call(functools.partial(comm_kernel, date_groups, row_groups), o...  44.4 us
    pallas_call x1, Pallas kernels, on_device(): pl.pallas_call(functools.partial(out_kernel, t_n * date_groups), grid=(ro...  7.71 us

profile of v1, /device:TPU:0, one launch (start us, length us, event | category | flops | bytes accessed | tf_op | source)
XLA Modules:
  0.0 52.8 jit_solution(9072585612801418947)
XLA Ops:
  0.6 44.4 %comm.1 = (f32[8,256,512]{2,1,0:T(8,128)}, f32[256,512]{1,0:T(8,128)}, f32[256,512]{1,0:T(8,128)}) custom-call(f32[8,256,512]{2,1,0:T(8,128)} %x.1), custom_call_target="tpu_custom_call" | custom-call | tf_op jit(solution)/shard_map/comm/pallas_call | solution.py:325
  45.1 7.7 %finish.1 = (f32[8,256,512]{2,1,0:T(8,128)}, f32[8,256,512]{2,1,0:T(8,128)}) custom-call(f32[8,256,512]{2,1,0:T(8,128)} %get-tuple-element.5.lm, f32[256,512]{1,0:T(8,128)} %get-tuple-element.6.tot, f32[256,512]{1,0:T(8,128)} %get-tuple-element.7.nxt), custom_call_target="tpu_custom_call" | custom-call | tf_op jit(solution)/shard_map/finish/pallas_call | solution.py:355

commit v2 on v1

--- a/solution.py
+++ b/solution.py
@@ -10,6 +10,7 @@
 RADIUS = 3
 RIM = 8
 CHUNK = 32
+HOP = 1
 MESH = pl.DeviceIdType.MESH
 NEAR = ((0, 1), (0, -1), (1, 0), (-1, 0), (1, 1), (1, -1), (-1, 1), (-1, -1), (2, 0), (-2, 0))
 
@@ -125,7 +126,6 @@
     @pl.when(has_prev)
     def _():
         suc[0].start()
-        suc[1].start()
 
     for c in loads:
         c.wait()
@@ -152,7 +152,7 @@
             lmv[t, pl.ds(base, CHUNK), :] = mean
             return acc + block[RIM : RIM + CHUNK] / mean
 
-        acc = lax.fori_loop(0, t_n, one, jnp.zeros((CHUNK, cols), jnp.float32))
+        acc = lax.fori_loop(0, t_n, one, jnp.zeros((CHUNK, cols), jnp.float32), unroll=4)
         part[pl.ds(base, CHUNK), :] = acc
 
     def away(k):
@@ -173,6 +173,7 @@
 
     @pl.when(has_prev)
     def _():
+        suc[1].start()
         suc[2].start()
         suc[3].start()
 
@@ -183,15 +184,6 @@
         @pl.when(up_row)
         def _():
             suc_up.start()
-
-    def second_half(k, _):
-        ratios(mine(k))
-        return 0
-
-    lax.fori_loop(0, n_half, second_half, 0)
-
-    mean_out = pltpu.make_async_copy(lmv, lm_out, out_sem.at[0])
-    mean_out.start()
 
     lead = jnp.where(a >= line // 2, 1, 0)
 
@@ -219,17 +211,36 @@
         place = pl.ds(mine(k), CHUNK)
         return remote(tot.at[place], tot.at[place], ag_s.at[k], ag_r.at[k], pair, r)
 
-    skew = 2
-    for i in range(n_half + skew):
-        if i < n_half:
+    edge = jnp.minimum(a, line - 1 - a)
+    lag = jnp.minimum(edge * HOP, n_half)
+    late = jnp.minimum((line - 1 - edge) * HOP, lag + n_half)
+
+    def turn(i, _):
+        @pl.when(i < n_half)
+        def _():
+            ratios(mine(i))
             rs_copy(i).wait_recv()
             own[i] = part[pl.ds(mine(i), CHUNK), :] + rsb[i]
-            scan(lead, i)
-        k = i - skew
-        if k >= 0:
+
+        j = i - lag
+
+        @pl.when((j >= 0) & (j < n_half))
+        def _():
+            scan(lead, j)
+
+        k = i - late
+
+        @pl.when((k >= 0) & (k < n_half))
+        def _():
             scan(1 - lead, k)
             tot[pl.ds(mine(k), CHUNK), :] = buf[0, k] + own[k] + buf[1, k]
             ag_copy(k).start()
+
+        return 0
+
+    lax.fori_loop(0, n_half + late, turn, 0)
+    mean_out = pltpu.make_async_copy(lmv, lm_out, out_sem.at[0])
+    mean_out.start()
 
     @pl.when(has_next)
     def _():
@@ -329,7 +340,7 @@
             jax.ShapeDtypeStruct((rows, cols), f32),
             jax.ShapeDtypeStruct((rows, cols), f32),
         ),
-        in_specs=[hbm],
+        in_specs=[pl.BlockSpec(memory_space=pltpu.HBM)],
         out_specs=(hbm, hbm, hbm),
         scratch_shapes=[
             vm(t_n, rows + 2 * RIM, cols),
@@ -346,10 +357,10 @@
             dma((n_half,)), dma((n_half,)), dma((2, n_half)), dma((2, n_half)),
             dma((n_half,)), dma((n_half,)), dma((3,)),
         ],
-        compiler_params=pltpu.CompilerParams(collective_id=0, has_side_effects=True),
+        compiler_params=pltpu.CompilerParams(collective_id=0, has_side_effects=True, vmem_limit_bytes=20 << 20),
         name="comm",
     )(intensity)
-    step = 32
+    step = 64
     big = pl.BlockSpec((t_n, step, cols), lambda i: (0, i, 0))
     flat = pl.BlockSpec((step, cols), lambda i: (i, 0))
     return pl.pallas_call(
@@ -361,6 +372,7 @@
         ),
         in_specs=[big, flat, flat],
         out_specs=(big, big),
+        compiler_params=pltpu.CompilerParams(vmem_limit_bytes=20 << 20),
         name="finish",
     )(lm, tot, nxt)
 

time: 53.1 us -> 43.8 us (0.82)
  Pallas kernels: 52.2 us -> 40.8 us
  local copies, waits for them, and re-layouts: 0 us -> 2.18 us
    pallas_call x1, Pallas kernels: 44.4 us -> 36.8 us  [on_device(): pl.pallas_call(functools.partial(comm_kernel, date_groups, row_groups), o...]
    pallas_call x1, Pallas kernels: 7.71 us -> 4.02 us  [on_device(): pl.pallas_call(functools.partial(out_kernel, t_n * date_groups), grid=(ro...]
    unnamed x0 -> x2, local copies, waits for them, and re-layouts: none -> 2.18 us
where the time goes in v2:
time: 43.8 us; the launch traced here: 43.6 us
  Pallas kernels  40.8 us (93%)
  local copies, waits for them, and re-layouts  2.18 us (5%)
  between operations  0.65 us (1%)
    pallas_call x1, Pallas kernels, on_device(): pl.pallas_call(functools.partial(comm_kernel, date_groups, row_groups), o...  36.8 us
    pallas_call x1, Pallas kernels, on_device(): pl.pallas_call(functools.partial(out_kernel, t_n * date_groups), grid=(ro...  4.02 us
    unnamed x2, local copies, waits for them, and re-layouts  2.18 us

profile of v2, /device:TPU:0, one launch (start us, length us, event | category | flops | bytes accessed | tf_op | source)
XLA Modules:
  0.0 43.6 jit_solution(12474819357937250091)
XLA Ops:
  0.6 0.0 copy-start
  0.6 2.2 %copy-done = f32[8,256,512]{2,1,0:T(8,128)S(1)} copy-done((f32[8,256,512]{2,1,0:T(8,128)S(1)}, f32[8,256,512]{2,1,0:T(8,128)}, u32[]{:S(2)}) %copy-start) | copy-done | bytes 4194328
  2.8 36.8 %comm.1 = (f32[8,256,512]{2,1,0:T(8,128)S(1)}, f32[256,512]{1,0:T(8,128)S(1)}, f32[256,512]{1,0:T(8,128)S(1)}) custom-call(f32[8,256,512]{2,1,0:T(8,128)S(1)} %copy-done), custom_call_target="tpu_custom_call" | custom-call | tf_op jit(solution)/shard_map/comm/pallas_call | solution.py:336
  39.6 4.0 %finish.1 = (f32[8,256,512]{2,1,0:T(8,128)}, f32[8,256,512]{2,1,0:T(8,128)}) custom-call(f32[8,256,512]{2,1,0:T(8,128)S(1)} %get-tuple-element.5.lm, f32[256,512]{1,0:T(8,128)S(1)} %get-tuple-element.6.tot, f32[256,512]{1,0:T(8,128)S(1)} %get-tuple-element.7.nxt), custom_call_target="tpu_custom_call" | custom-call | tf_op jit(solution)/shard_map/finish/pallas_call | solution.py:366
Async XLA Ops:
  0.6 2.2 %copy-start = (f32[8,256,512]{2,1,0:T(8,128)S(1)}, f32[8,256,512]{2,1,0:T(8,128)}, u32[]{:S(2)}) copy-start(f32[8,256,512]{2,1,0:T(8,128)} %x.1) | copy-start | bytes 12582916

commit v3 on v2

--- a/solution.py
+++ b/solution.py
@@ -11,6 +11,10 @@
 RIM = 8
 CHUNK = 32
 HOP = 1
+N_SUC = 8
+EARLY_ODD = 4
+EARLY_EVEN = 4
+PER = 1
 MESH = pl.DeviceIdType.MESH
 NEAR = ((0, 1), (0, -1), (1, 0), (-1, 0), (1, 1), (1, -1), (-1, 1), (-1, -1), (2, 0), (-2, 0))
 
@@ -37,11 +41,12 @@
     return (high - low + 1).astype(jnp.float32)
 
 
-def comm_kernel(dates_n, rows_n_groups, x, lm_out, tot_out, nxt_out,
-                xv, sv, lmv, part, rsb, own, buf, fwd, tot, nxt,
+def comm_kernel(dates_n, rows_n_groups, x, lmv, tot_out, nxt,
+                xv, sv, part, rsb, own, buf, fwd, tot,
                 load_sem, rim_s, rim_r, suc_s, suc_r, rs_s, rs_r, sc_s, sc_r,
-                ag_s, ag_r, out_sem):
+                ag_s, ag_r):
     t_n, rows, cols = x.shape
+    n_suc = suc_s.shape[0] - 2
     half = rows // 2
     n_half = half // CHUNK
     line = dates_n // 2
@@ -111,13 +116,13 @@
     def _():
         rim_up.start()
 
-    n_suc = 4
     piece = rows // n_suc
-    suc = [
-        remote(x.at[0, pl.ds(i * piece, piece)], sv.at[pl.ds(RIM + i * piece, piece)],
-               suc_s.at[i], suc_r.at[i], d - 1, r)
-        for i in range(n_suc)
-    ]
+
+    def suc_copy(i):
+        place = pl.multiple_of(i * piece, RIM)
+        return remote(x.at[0, pl.ds(place, piece)], sv.at[pl.ds(RIM + place, piece)],
+                      suc_s.at[i], suc_r.at[i], d - 1, r)
+
     suc_down = remote(x.at[0, pl.ds(rows - RIM, RIM)], sv.at[pl.ds(0, RIM)],
                       suc_s.at[n_suc], suc_r.at[n_suc], d - 1, r + 1)
     suc_up = remote(x.at[0, pl.ds(0, RIM)], sv.at[pl.ds(RIM + rows, RIM)],
@@ -125,7 +130,13 @@
 
     @pl.when(has_prev)
     def _():
-        suc[0].start()
+        for i in range(EARLY_ODD):
+            suc_copy(i).start()
+
+    @pl.when(has_prev & (b == 0))
+    def _():
+        for i in range(EARLY_ODD, EARLY_EVEN):
+            suc_copy(i).start()
 
     for c in loads:
         c.wait()
@@ -173,9 +184,10 @@
 
     @pl.when(has_prev)
     def _():
-        suc[1].start()
-        suc[2].start()
-        suc[3].start()
+        @pl.when(b == 1)
+        def _():
+            for i in range(EARLY_ODD, n_suc):
+                suc_copy(i).start()
 
         @pl.when(down_row)
         def _():
@@ -228,6 +240,11 @@
         def _():
             scan(lead, j)
 
+            @pl.when(has_prev & (b == 0))
+            def _():
+                for m in range(PER):
+                    suc_copy(EARLY_EVEN + PER * j + m).start()
+
         k = i - late
 
         @pl.when((k >= 0) & (k < n_half))
@@ -239,13 +256,10 @@
         return 0
 
     lax.fori_loop(0, n_half + late, turn, 0)
-    mean_out = pltpu.make_async_copy(lmv, lm_out, out_sem.at[0])
-    mean_out.start()
-
     @pl.when(has_next)
     def _():
-        for c in suc:
-            c.wait_recv()
+        for i in range(n_suc):
+            suc_copy(i).wait_recv()
 
         @pl.when(up_row)
         def _():
@@ -267,17 +281,13 @@
     def _():
         nxt[...] = lmv[t_n - 1]
 
-    nxt_copy = pltpu.make_async_copy(nxt, nxt_out, out_sem.at[1])
-    nxt_copy.start()
-
     def ag_arrival(k):
         place = pl.ds(away(k), CHUNK)
         return remote(tot.at[place], tot.at[place], ag_s.at[k], ag_r.at[k], pair, r)
 
     for k in range(n_half):
         ag_arrival(k).wait_recv()
-    tot_copy = pltpu.make_async_copy(tot, tot_out, out_sem.at[2])
-    tot_copy.start()
+    tot_out[...] = tot[...]
 
     @pl.when(down_row)
     def _():
@@ -289,8 +299,8 @@
 
     @pl.when(has_prev)
     def _():
-        for c in suc:
-            c.wait_send()
+        for i in range(n_suc):
+            suc_copy(i).wait_send()
 
         @pl.when(down_row)
         def _():
@@ -308,10 +318,6 @@
             @pl.when(goes(way))
             def _():
                 scan_copy(way, k).wait_send()
-
-    mean_out.wait()
-    nxt_copy.wait()
-    tot_copy.wait()
 
 
 def out_kernel(total_dates, lm, tot, nxt, filtered, change):
@@ -336,28 +342,26 @@
     lm, tot, nxt = pl.pallas_call(
         functools.partial(comm_kernel, date_groups, row_groups),
         out_shape=(
-            jax.ShapeDtypeStruct((t_n, rows, cols), f32),
-            jax.ShapeDtypeStruct((rows, cols), f32),
-            jax.ShapeDtypeStruct((rows, cols), f32),
+            vm(t_n, rows, cols),
+            vm(rows, cols),
+            vm(rows, cols),
         ),
         in_specs=[pl.BlockSpec(memory_space=pltpu.HBM)],
-        out_specs=(hbm, hbm, hbm),
+        out_specs=(pl.BlockSpec(memory_space=pltpu.VMEM),) * 3,
         scratch_shapes=[
             vm(t_n, rows + 2 * RIM, cols),
             vm(rows + 2 * RIM, cols),
-            vm(t_n, rows, cols),
             vm(rows, cols),
             vm(n_half, CHUNK, cols),
             vm(n_half, CHUNK, cols),
             vm(2, n_half, CHUNK, cols),
             vm(2, n_half, CHUNK, cols),
             vm(rows, cols),
-            vm(rows, cols),
-            dma((t_n,)), dma((2,)), dma((2,)), dma((6,)), dma((6,)),
+            dma((t_n,)), dma((2,)), dma((2,)), dma((2 + N_SUC,)), dma((2 + N_SUC,)),
             dma((n_half,)), dma((n_half,)), dma((2, n_half)), dma((2, n_half)),
-            dma((n_half,)), dma((n_half,)), dma((3,)),
+            dma((n_half,)), dma((n_half,)),
         ],
-        compiler_params=pltpu.CompilerParams(collective_id=0, has_side_effects=True, vmem_limit_bytes=20 << 20),
+        compiler_params=pltpu.CompilerParams(collective_id=0, has_side_effects=True, vmem_limit_bytes=57 << 20),
         name="comm",
     )(intensity)
     step = 64

time: 43.8 us -> 39.3 us (0.90)
  Pallas kernels: 40.8 us -> 38.5 us
  local copies, waits for them, and re-layouts: 2.18 us -> 0 us
    pallas_call x1, Pallas kernels: 36.8 us -> 34.5 us  [on_device(): pl.pallas_call(functools.partial(comm_kernel, date_groups, row_groups), o...]
    unnamed x2 -> x0, local copies, waits for them, and re-layouts: 2.18 us -> none
where the time goes in v3:
time: 39.3 us; the launch traced here: 39.2 us
  Pallas kernels  38.5 us (98%)
  between operations  0.64 us (2%)
    pallas_call x1, Pallas kernels, on_device(): pl.pallas_call(functools.partial(comm_kernel, date_groups, row_groups), o...  34.5 us
    pallas_call x1, Pallas kernels, on_device(): pl.pallas_call(functools.partial(out_kernel, t_n * date_groups), grid=(ro...  4.02 us

profile of v3, /device:TPU:0, one launch (start us, length us, event | category | flops | bytes accessed | tf_op | source)
XLA Modules:
  0.0 39.2 jit_solution(16720193004990718339)
XLA Ops:
  0.6 34.5 %comm.1 = (f32[8,256,512]{2,1,0:T(8,128)S(1)}, f32[256,512]{1,0:T(8,128)S(1)}, f32[256,512]{1,0:T(8,128)S(1)}) custom-call(f32[8,256,512]{2,1,0:T(8,128)} %x.1), custom_call_target="tpu_custom_call" | custom-call | tf_op jit(solution)/shard_map/comm/pallas_call | solution.py:342
  35.2 4.0 %finish.1 = (f32[8,256,512]{2,1,0:T(8,128)}, f32[8,256,512]{2,1,0:T(8,128)}) custom-call(f32[8,256,512]{2,1,0:T(8,128)S(1)} %get-tuple-element.5.lm, f32[256,512]{1,0:T(8,128)S(1)} %get-tuple-element.6.tot, f32[256,512]{1,0:T(8,128)S(1)} %get-tuple-element.7.nxt), custom_call_target="tpu_custom_call" | custom-call | tf_op jit(solution)/shard_map/finish/pallas_call | solution.py:370

commit v4 on v3

--- a/solution.py
+++ b/solution.py
@@ -11,10 +11,6 @@
 RIM = 8
 CHUNK = 32
 HOP = 1
-N_SUC = 8
-EARLY_ODD = 4
-EARLY_EVEN = 4
-PER = 1
 MESH = pl.DeviceIdType.MESH
 NEAR = ((0, 1), (0, -1), (1, 0), (-1, 0), (1, 1), (1, -1), (-1, 1), (-1, -1), (2, 0), (-2, 0))
 
@@ -130,12 +126,7 @@
 
     @pl.when(has_prev)
     def _():
-        for i in range(EARLY_ODD):
-            suc_copy(i).start()
-
-    @pl.when(has_prev & (b == 0))
-    def _():
-        for i in range(EARLY_ODD, EARLY_EVEN):
+        for i in range(n_half):
             suc_copy(i).start()
 
     for c in loads:
@@ -186,7 +177,7 @@
     def _():
         @pl.when(b == 1)
         def _():
-            for i in range(EARLY_ODD, n_suc):
+            for i in range(n_half, n_suc):
                 suc_copy(i).start()
 
         @pl.when(down_row)
@@ -242,8 +233,7 @@
 
             @pl.when(has_prev & (b == 0))
             def _():
-                for m in range(PER):
-                    suc_copy(EARLY_EVEN + PER * j + m).start()
+                suc_copy(n_half + j).start()
 
         k = i - late
 
@@ -357,7 +347,7 @@
             vm(2, n_half, CHUNK, cols),
             vm(2, n_half, CHUNK, cols),
             vm(rows, cols),
-            dma((t_n,)), dma((2,)), dma((2,)), dma((2 + N_SUC,)), dma((2 + N_SUC,)),
+            dma((t_n,)), dma((2,)), dma((2,)), dma((2 + 2 * n_half,)), dma((2 + 2 * n_half,)),
             dma((n_half,)), dma((n_half,)), dma((2, n_half)), dma((2, n_half)),
             dma((n_half,)), dma((n_half,)),
         ],

time: 39.3 us -> 39.3 us (level)
  no operation moved by 1% of the time
where the time goes in v4:
time: 39.3 us; the launch traced here: 39.2 us
  Pallas kernels  38.5 us (98%)
  between operations  0.64 us (2%)
    pallas_call x1, Pallas kernels, on_device(): pl.pallas_call(functools.partial(comm_kernel, date_groups, row_groups), o...  34.5 us
    pallas_call x1, Pallas kernels, on_device(): pl.pallas_call(functools.partial(out_kernel, t_n * date_groups), grid=(ro...  4.02 us

profile of v4, /device:TPU:0, one launch (start us, length us, event | category | flops | bytes accessed | tf_op | source)
XLA Modules:
  0.0 39.2 jit_solution(16720193004990718339)
XLA Ops:
  0.6 34.5 %comm.1 = (f32[8,256,512]{2,1,0:T(8,128)S(1)}, f32[256,512]{1,0:T(8,128)S(1)}, f32[256,512]{1,0:T(8,128)S(1)}) custom-call(f32[8,256,512]{2,1,0:T(8,128)} %x.1), custom_call_target="tpu_custom_call" | custom-call | tf_op jit(solution)/shard_map/comm/pallas_call | solution.py:332
  35.2 4.0 %finish.1 = (f32[8,256,512]{2,1,0:T(8,128)}, f32[8,256,512]{2,1,0:T(8,128)}) custom-call(f32[8,256,512]{2,1,0:T(8,128)S(1)} %get-tuple-element.5.lm, f32[256,512]{1,0:T(8,128)S(1)} %get-tuple-element.6.tot, f32[256,512]{1,0:T(8,128)S(1)} %get-tuple-element.7.nxt), custom_call_target="tpu_custom_call" | custom-call | tf_op jit(solution)/shard_map/finish/pallas_call | solution.py:360
